TPU v7x, 32 devices: a whole 2x2x4 slice. The times are simulated.
32 devices in a mesh: grid: 8 (over z, y), bead: 4 (over x, core).
Axes of the slice: x: 2, y: 2, z: 4, core: 2. Of those that a mesh axis runs over, the one named last changes fastest.
Arguments:
- positions: float32 [3, 32, 4096], P(None, 'bead', 'grid'), may hold values from -6 to 6
- momenta: float32 [3, 32, 4096], P(None, 'bead', 'grid'), may hold values from -6 to 6
- noise: float32 [3, 32, 4096], P(None, 'bead', 'grid'), may hold values from -6 to 6
- charges: float32 [4096], P('grid'), may hold values from -5 to 5
- slab_route: int32 [4096, 1], P('grid'), may hold values from 0 to 7; in each aligned block of 512 rows (0 to 511, 512 to 1023, ...) at most 128 rows name the same one
- cells: int32 [3, 4096], P(None, 'grid'), may hold values from 0 to 255, as said below
- offsets: float32 [3, 4096], P(None, 'grid'), may hold values from 0 to 0.999
- nbr_tiles: int32 [32, 4], P('grid'), may hold values from 0 to 3
Outputs:
- new_positions: float32 [3, 32, 4096], P(None, 'bead', 'grid')
- new_momenta: float32 [3, 32, 4096], P(None, 'bead', 'grid')
Inputs may be any that keep to these rules, and one draw needn't show every extreme that they name: `slab_route`: among the 512 atoms of one domain at most 128 name the same slab, a bound that some block reaches of them. `cells`: row 0 lies below 32, row 1 below 256, row 2 below 256. `nbr_tiles`: tile numbers within the domain of the listing tile.
All inputs are finite; a program needn't handle non-finite values.
Results may differ from a plain program's by a relative error of at most 0.0003.
Values sent between devices are 32-bit elements; how exact they have to be, the bound alone decides.
A program may use at most 64 MiB of HBM per device.

v0:
```python
import math

import jax
import jax.numpy as jnp
from jax import lax
from jax.sharding import PartitionSpec as P

GX = 256
GY = 256
GZ = 256
BEADS = 32
TILE = 128
NBR = 4


highest = lax.Precision.HIGHEST
time_step = 0.5
polymer_frequency = 1.0
centroid_friction = 0.5
coulomb_scale = 100000.0
screen_width = 200.0
pair_strength = 1.0 / 128.0
pair_range = 4.0


def with_halo(cells, sides, width):
    for axis, dim in sides:
        count = lax.axis_size(axis)
        head = lax.slice_in_dim(cells, 0, width, axis=dim)
        tail = lax.slice_in_dim(cells, cells.shape[dim] - width, cells.shape[dim], axis=dim)
        cells = jnp.concatenate(
            [
                lax.ppermute(tail, axis, [(i, (i + 1) % count) for i in range(count)]),
                cells,
                lax.ppermute(head, axis, [((i + 1) % count, i) for i in range(count)]),
            ],
            axis=dim,
        )
    return cells


def spline(fraction):
    remain = 1.0 - fraction
    square = fraction * fraction
    cubic = square * fraction
    values = [
        remain * remain * remain / 6.0,
        (3.0 * cubic - 6.0 * square + 4.0) / 6.0,
        (-3.0 * cubic + 3.0 * square + 3.0 * fraction + 1.0) / 6.0,
        cubic / 6.0,
    ]
    slopes = [
        -0.5 * remain * remain,
        0.5 * (3.0 * square - 4.0 * fraction),
        0.5 * (-3.0 * square + 2.0 * fraction + 1.0),
        0.5 * square,
    ]
    return (values, slopes)


def influence(index_x, index_y, index_z):
    wave_x = ((index_x + GX // 2) % GX - GX // 2).astype(jnp.float32)
    wave_y = ((index_y + GY // 2) % GY - GY // 2).astype(jnp.float32)
    wave_z = ((index_z + GZ // 2) % GZ - GZ // 2).astype(jnp.float32)
    wave_square = wave_x * wave_x + wave_y * wave_y + wave_z * wave_z
    centre = wave_square == 0.0
    safe_square = jnp.where(centre, 1.0, wave_square)
    return jnp.where(
        centre,
        0.0,
        coulomb_scale * jnp.exp(-wave_square / (2.0 * screen_width * screen_width)) / safe_square,
    )


def pair_force(centre, beside_all):
    separation = centre[:, :, :, None] - beside_all[:, :, None, :]
    distance_sq = jnp.sum(separation * separation, axis=0)
    weight = pair_strength * jnp.exp(-distance_sq / pair_range)
    return jnp.sum(weight[None] * separation, axis=3)


def domain_force(local_positions, neighbours):
    tile_count = neighbours.shape[0]
    bead_total = local_positions.shape[1]
    shaped = local_positions.reshape(3, bead_total, tile_count, TILE)

    def one_tile(tile_index):
        centre = lax.dynamic_index_in_dim(shaped, tile_index, 2, keepdims=False)
        beside_all = jnp.take(shaped, neighbours[tile_index], axis=2).reshape(
            3, bead_total, NBR * TILE
        )
        return pair_force(centre, beside_all)

    forces = lax.map(one_tile, jnp.arange(tile_count, dtype=jnp.int32))
    return jnp.moveaxis(forces, 0, 2).reshape(3, bead_total, tile_count * TILE)


def mode_matrix(bead_total):
    mode_index = jnp.arange(bead_total, dtype=jnp.int32)[:, None]
    bead_index = jnp.arange(bead_total, dtype=jnp.int32)[None, :]
    angle = (mode_index * bead_index % bead_total).astype(jnp.float32) * (
        2.0 * math.pi / bead_total
    )
    middle = bead_total // 2
    first = jnp.full(angle.shape, 1.0 / math.sqrt(bead_total), jnp.float32)
    scaled = math.sqrt(2.0 / bead_total)
    return jnp.where(
        mode_index == 0,
        first,
        jnp.where(
            mode_index < middle,
            scaled * jnp.cos(angle),
            jnp.where(
                mode_index == middle,
                jnp.cos(angle) / math.sqrt(bead_total),
                scaled * jnp.sin(angle),
            ),
        ),
    )


def evolve(position_modes, momentum_modes, kicks, mode_index, bead_total):
    frequency = (
        2.0 * polymer_frequency * jnp.sin(mode_index.astype(jnp.float32) * (math.pi / bead_total))
    )[None, :, None]
    centroid = (mode_index == 0)[None, :, None]
    half_step = 0.5 * time_step
    cosine_term = jnp.cos(frequency * half_step)
    sine_term = jnp.sin(frequency * half_step)
    safe_frequency = jnp.where(centroid, 1.0, frequency)
    drift_factor = jnp.where(centroid, half_step, sine_term / safe_frequency)

    def rotate(moved_q, moved_p):
        return (
            moved_q * cosine_term + moved_p * drift_factor,
            moved_p * cosine_term - moved_q * frequency * sine_term,
        )

    position_modes, momentum_modes = rotate(position_modes, momentum_modes)
    friction = jnp.where(centroid, centroid_friction, 2.0 * frequency)
    damping = jnp.exp(-friction * time_step)
    momentum_modes = damping * momentum_modes + jnp.sqrt(1.0 - damping * damping) * kicks
    return rotate(position_modes, momentum_modes)


def grid_positions(target, cells, offsets, planes):
    first = (target * planes + cells[0]).astype(jnp.float32) + offsets[0]
    second = cells[1].astype(jnp.float32) + offsets[1]
    third = cells[2].astype(jnp.float32) + offsets[2]
    return jnp.stack([first, second, third])


def spread_table(lowest_line, values, grid_rows, length, first_offset):
    weights_table = jnp.zeros((grid_rows.shape[0], lowest_line.shape[0]), jnp.float32)
    for offset in range(4):
        target_cell = lowest_line + (offset + first_offset)
        if length > 0:
            target_cell = target_cell % length
        matches = grid_rows[:, None] == target_cell[None, :]
        weights_table = weights_table + jnp.where(matches, values[offset][None, :], 0.0)
    return weights_table


def dft_tables(length):
    sample = jnp.arange(length, dtype=jnp.int32)
    angle = (sample[:, None] * sample[None, :] % length).astype(jnp.float32) * (
        2.0 * math.pi / length
    )
    return (jnp.cos(angle), jnp.sin(angle))


def complex_pass(spectrum, cosine, sine_table, direction, pattern):
    real_in = spectrum[0]
    imag_in = spectrum[1]
    real_out = jnp.einsum(pattern, cosine, real_in, precision=highest) - direction * jnp.einsum(
        pattern, sine_table, imag_in, precision=highest
    )
    imag_out = jnp.einsum(pattern, cosine, imag_in, precision=highest) + direction * jnp.einsum(
        pattern, sine_table, real_in, precision=highest
    )
    return jnp.stack([real_out, imag_out])


def per_device(positions, momenta, noise, charges, slab_route, cells, offsets, nbr_tiles):
    grid_count = lax.axis_size("grid")
    bead_count = lax.axis_size("bead")
    grid_rank = lax.axis_index("grid")
    bead_rank = lax.axis_index("bead")
    atom_count = charges.shape[0]
    planes = GX // grid_count
    rows_local = GY // bead_count
    depth_local = GZ // bead_count
    rows_split = GY // grid_count
    capacity = 2 * atom_count // grid_count
    beads_local = positions.shape[1]
    short_force = domain_force(positions, nbr_tiles)
    target = slab_route[:, 0]
    grid_pos = grid_positions(target, cells, offsets, planes)
    onehot_slab = (target[:, None] == jnp.arange(grid_count, dtype=jnp.int32)[None, :]).astype(
        jnp.int32
    )
    order_in = jnp.sum(jnp.cumsum(onehot_slab, axis=0) * onehot_slab, axis=1) - 1
    slot_index = target * capacity + order_in
    fields = jnp.concatenate([charges[None, :], grid_pos], axis=0)
    outgoing = jnp.zeros((4, grid_count * capacity), jnp.float32).at[:, slot_index].set(fields)
    incoming = lax.all_to_all(
        outgoing.reshape(4, grid_count, capacity), "grid", split_axis=1, concat_axis=1, tiled=True
    )
    incoming = incoming.reshape(4, grid_count * capacity)
    got_charge = incoming[0]
    lowest = jnp.floor(incoming[1:])
    fraction = incoming[1:] - lowest
    lowest_int = lowest.astype(jnp.int32)
    values, slopes = spline(fraction)
    pad_rows = jnp.arange(planes + 3, dtype=jnp.int32)
    row_index = bead_rank * rows_local + jnp.arange(rows_local, dtype=jnp.int32)
    depth_index = jnp.arange(GZ, dtype=jnp.int32)
    local_lowest = lowest_int[0] - grid_rank * planes
    plane_weight = spread_table(local_lowest, [member[0] for member in values], pad_rows, 0, 0)
    plane_slope = spread_table(local_lowest, [member[0] for member in slopes], pad_rows, 0, 0)
    row_weight = spread_table(lowest_int[1], [member[1] for member in values], row_index, GY, -1)
    row_slope = spread_table(lowest_int[1], [member[1] for member in slopes], row_index, GY, -1)
    depth_weight = spread_table(
        lowest_int[2], [member[2] for member in values], depth_index, GZ, -1
    )
    depth_slope = spread_table(lowest_int[2], [member[2] for member in slopes], depth_index, GZ, -1)
    charged_planes = plane_weight * got_charge[None, :]

    def spread_plane(plane_index, running):
        weighted = (
            row_weight
            * lax.dynamic_index_in_dim(charged_planes, plane_index, 0, keepdims=False)[None, :]
        )
        layer_values = jnp.einsum("yr,zr->yz", weighted, depth_weight, precision=highest)
        return lax.dynamic_update_index_in_dim(running, layer_values, plane_index, 0)

    padded = lax.fori_loop(
        0, planes + 3, spread_plane, jnp.zeros((planes + 3, rows_local, GZ), jnp.float32)
    )
    extended = with_halo(padded, (("grid", 0),), 2)
    own_planes = extended[3 : planes + 3]
    charge_grid = own_planes.at[0:2].add(extended[0:2]).at[planes - 1].add(extended[planes + 5])
    cos_x, sin_x = dft_tables(GX)
    cos_y, sin_y = dft_tables(GY)
    cos_z, sin_z = dft_tables(GZ)
    real_part = jnp.einsum("xyz,zk->yxk", charge_grid, cos_z, precision=highest)
    imag_part = -jnp.einsum("xyz,zk->yxk", charge_grid, sin_z, precision=highest)
    spectrum = lax.all_to_all(
        jnp.stack([real_part, imag_part]), "bead", split_axis=3, concat_axis=1, tiled=True
    )
    spectrum = complex_pass(spectrum, cos_y, sin_y, -1.0, "ky,yxz->xkz")
    spectrum = lax.all_to_all(spectrum, "grid", split_axis=2, concat_axis=1, tiled=True)
    spectrum = complex_pass(spectrum, cos_x, sin_x, -1.0, "kx,xyz->kyz")
    screen = influence(
        jnp.arange(GX, dtype=jnp.int32)[:, None, None],
        (grid_rank * rows_split + jnp.arange(rows_split, dtype=jnp.int32))[None, :, None],
        (bead_rank * depth_local + jnp.arange(depth_local, dtype=jnp.int32))[None, None, :],
    )
    spectrum = spectrum * (screen / float(GX * GY * GZ))[None]
    spectrum = complex_pass(spectrum, cos_x, sin_x, 1.0, "kx,xyz->kyz")
    spectrum = lax.all_to_all(spectrum, "grid", split_axis=1, concat_axis=2, tiled=True)
    spectrum = complex_pass(spectrum, cos_y, sin_y, 1.0, "ky,xyz->kxz")
    spectrum = lax.all_to_all(spectrum, "bead", split_axis=1, concat_axis=3, tiled=True)
    potential = jnp.einsum("yxk,kz->xyz", spectrum[0], cos_z, precision=highest) - jnp.einsum(
        "yxk,kz->xyz", spectrum[1], sin_z, precision=highest
    )
    near_potential = with_halo(potential, (("grid", 0),), 2)[1:]

    def gather_plane(plane_index, totals):
        layer_values = lax.dynamic_index_in_dim(near_potential, plane_index, 0, keepdims=False)
        along_rows = jnp.einsum("yz,yr->zr", layer_values, row_weight, precision=highest)
        along_slope = jnp.einsum("yz,yr->zr", layer_values, row_slope, precision=highest)
        plain_sum = jnp.sum(along_rows * depth_weight, axis=0)
        depth_term = jnp.sum(along_rows * depth_slope, axis=0)
        row_term = jnp.sum(along_slope * depth_weight, axis=0)
        weight_here = lax.dynamic_index_in_dim(plane_weight, plane_index, 0, keepdims=False)
        slope_here = lax.dynamic_index_in_dim(plane_slope, plane_index, 0, keepdims=False)
        return (
            totals[0] + slope_here * plain_sum,
            totals[1] + weight_here * row_term,
            totals[2] + weight_here * depth_term,
        )

    empty_sum = jnp.zeros_like(got_charge)
    force_x, force_y, force_z = lax.fori_loop(
        0, planes + 3, gather_plane, (empty_sum, empty_sum, empty_sum)
    )
    slot_force = -got_charge[None, :] * jnp.stack([force_x, force_y, force_z])
    returned = lax.all_to_all(
        slot_force.reshape(3, grid_count, capacity), "grid", split_axis=1, concat_axis=1, tiled=True
    )
    returned = returned.reshape(3, grid_count * capacity)
    mesh_force = lax.psum(returned[:, slot_index], "bead")
    kicked = momenta + 0.5 * time_step * (short_force + mesh_force[:, None, :])
    matrix = mode_matrix(BEADS)
    all_positions, all_momenta = (
        lax.all_gather(positions, "bead", axis=1, tiled=True),
        lax.all_gather(kicked, "bead", axis=1, tiled=True),
    )
    own_rows = lax.dynamic_slice_in_dim(matrix, bead_rank * beads_local, beads_local, 0)
    mode_index = bead_rank * beads_local + jnp.arange(beads_local, dtype=jnp.int32)
    position_modes = jnp.einsum("kb,cba->cka", own_rows, all_positions, precision=highest)
    momentum_modes = jnp.einsum("kb,cba->cka", own_rows, all_momenta, precision=highest)
    position_modes, momentum_modes = evolve(
        position_modes, momentum_modes, noise, mode_index, BEADS
    )
    share_q = jnp.einsum("kb,cka->cba", own_rows, position_modes, precision=highest)
    share_p = jnp.einsum("kb,cka->cba", own_rows, momentum_modes, precision=highest)
    new_positions, new_momenta = (
        lax.psum_scatter(share_q, "bead", scatter_dimension=1, tiled=True),
        lax.psum_scatter(share_p, "bead", scatter_dimension=1, tiled=True),
    )
    return (new_positions, new_momenta)


def solution(mesh):
    in_specs = (
        P(None, "bead", "grid"),
        P(None, "bead", "grid"),
        P(None, "bead", "grid"),
        P("grid"),
        P("grid", None),
        P(None, "grid"),
        P(None, "grid"),
        P("grid", None),
    )
    out_specs = (P(None, "bead", "grid"), P(None, "bead", "grid"))
    return jax.shard_map(
        per_device, mesh=mesh, in_specs=in_specs, out_specs=out_specs, check_vma=False
    )
```

profile of v0, /device:TPU:0, one launch (start us, length us, event | category | flops | bytes accessed | tf_op | source)
XLA Modules:
  0.0 1099.0 jit_solution(13626405696710225203)
XLA Ops:
  15.0 7.3 all-to-all-start
  22.4 6.5 all-to-all-done
  31.8 51.6 %while.47 = (s32[]{:T(128)}, f32[35,64,256]{2,1,0:T(8,128)S(1)}, f32[35,1024]{1,0:T(8,128)S(1)}, s32[1024]{0:T(1024)S(1)}, f32[1024]{0:T(1024)S(1)}, /*index=5*/...) while((s32[]{:T(128)}, f32[35,64,256]{2,1,0:T(8,128)S(1)}, ...), condition=%wide.region_9.10_spmd.clone, body=%wide.region_8.9_spmd.clone.sunk | while | flops 204996608 | bytes 144069 | solution.py:237
  84.5 4.6 collective-permute-start.1
  99.7 9.2 copy.101
  108.9 8.7 reshape.456
  117.6 53.8 %all_to_all.70 = f32[4,1,262144]{2,1,0:T(1,128)} all-to-all(f32[4,1,262144]{2,1,0:T(1,128)} %reshape.456), channel_id=1, replica_groups=mesh['grid'=8,'bead'=4] {'bead'}, dimensions={0} | all-to-all | bytes 8388608 | tf_op jit(solution)/shard_map/all_to_all | solution.py:248
  172.0 27.1 %reduce.6 = f32[4,262144]{1,0:T(4,128)} reduce(f32[4,1,262144]{2,1,0:T(1,128)} %all_to_all.70, f32[]{:T(128)} %broadcast.898), dimensions={1}, to_apply=%all_to_all.51.reduce_sub_computation | reduce | bytes 8388612 | tf_op jit(solution)/shard_map/all_to_all | solution.py:248
  199.1 9.3 reshape.457
  208.5 12.1 %copy.130 = f32[2,64,32,4,64]{1,3,4,2,0:T(4,128)} copy(f32[2,64,32,4,64]{1,2,0,4,3:T(8,128)} %bitcast.345) | data formatting | bytes 8388608 | tf_op jit(solution)/shard_map/all_to_all | solution.py:248
  220.5 7.8 fusion.295
  236.6 5.7 squeeze.79
  242.3 4.6 fusion.108
  254.9 9.2 copy.103
  264.1 9.9 reshape.458
  273.9 6.4 all-to-all-start.2
  282.6 90.7 %all-to-all-done.2 = f32[8,1,131072]{2,1,0:T(1,128)} async-done(((f32[8,1,131072]{2,1,0:T(1,128)}), f32[8,1,131072]{2,1,0:T(1,128)}, u32[]{:S(2)}, u32[]{:S(2)}) %all-to-all-start.2) | async-done | bytes 4194336 | tf_op jit(solution)/shard_map/all_to_all | solution.py:252
  373.3 14.0 %reduce.7 = f32[8,131072]{1,0:T(8,128)} reduce(f32[8,1,131072]{2,1,0:T(1,128)} %all-to-all-done.2, f32[]{:T(128)} %broadcast.898), dimensions={1}, to_apply=%all_to_all.54.reduce_sub_computation | reduce | bytes 8388612 | tf_op jit(solution)/shard_map/all_to_all | solution.py:252
  387.3 8.8 reshape.459
  396.1 8.2 copy.104
  413.9 4.2 fusion.145
  418.1 4.2 fusion.127
  453.9 9.2 copy.111
  463.1 9.9 reshape.460
  473.0 4.8 all-to-all-start.3
  477.8 92.5 %all-to-all-done.3 = f32[8,1,131072]{2,1,0:T(1,128)} async-done(((f32[8,1,131072]{2,1,0:T(1,128)}), f32[8,1,131072]{2,1,0:T(1,128)}, u32[]{:S(2)}, u32[]{:S(2)}) %all-to-all-start.3) | async-done | bytes 4194336 | tf_op jit(solution)/shard_map/all_to_all | solution.py:261
  570.3 13.8 %reduce.8 = f32[8,131072]{1,0:T(8,128)} reduce(f32[8,1,131072]{2,1,0:T(1,128)} %all-to-all-done.3, f32[]{:T(128)} %broadcast.898), dimensions={1}, to_apply=%all_to_all.57.reduce_sub_computation | reduce | bytes 8388612 | tf_op jit(solution)/shard_map/all_to_all | solution.py:261
  584.1 8.8 reshape.461
  592.9 4.4 copy.112
  606.0 4.2 fusion.149
  630.4 9.2 copy.119
  639.6 8.7 reshape.462
  648.3 5.0 all-to-all-start.4
  653.3 24.9 %while.46 = (s32[]{:T(128)}, f32[4,3,8,128]{3,2,1,0:T(8,128)S(1)}, s32[4]{0:T(128)S(1)}, f32[3,8,4,128]{3,1,2,0:T(8,128)S(1)}, s32[4,4]{1,0:T(4,128)S(1)}, /*index=5*/s32[]{:T(128)}, s32[]{:T(128)}, s32[]{:T(128)}) while((s32[]{:T(128)}, f32[4,3,8,128]{3,2,1,0:T(8,128)S(1)}, s32[4]{0:T(128)S(1)}, f32[3,8,4,128]{3,1,2,0:T(8,128)S(1)}, ...), condition=%wide.region_3.4_spmd, body=%wide.region_0.3_spmd.sunk | while | flops 10496041 | bytes 8774891 | solution.py:94
  678.6 22.9 %all-to-all-done.4 = f32[4,1,262144]{2,1,0:T(1,128)} async-done(((f32[4,1,262144]{2,1,0:T(1,128)}), f32[4,1,262144]{2,1,0:T(1,128)}, u32[]{:S(2)}, u32[]{:S(2)}) %all-to-all-start.4) | async-done | bytes 4194336 | tf_op jit(solution)/shard_map/all_to_all | solution.py:263
  701.5 15.5 %reduce.9 = f32[4,262144]{1,0:T(4,128)} reduce(f32[4,1,262144]{2,1,0:T(1,128)} %all-to-all-done.4, f32[]{:T(128)} %broadcast.898), dimensions={1}, to_apply=%all_to_all.60.reduce_sub_computation | reduce | bytes 8388612 | tf_op jit(solution)/shard_map/all_to_all | solution.py:263
  717.0 9.3 reshape.463
  726.4 12.1 %copy.129 = f32[2,4,64,32,64]{4,1,2,3,0:T(4,128)} copy(f32[2,4,64,32,64]{4,3,0,2,1:T(8,128)} %bitcast.348) | data formatting | bytes 8388608 | tf_op jit(solution)/shard_map/all_to_all | solution.py:263
  738.4 7.7 fusion.292
  746.2 4.5 squeeze.86
  759.1 4.5 subtract_bitcast_fusion
  774.5 240.1 %while.48 = (s32[]{:T(128)}, f32[1024]{0:T(1024)S(1)}, f32[1024]{0:T(1024)S(1)}, f32[1024]{0:T(1024)S(1)}, f32[35,1024]{1,0:T(8,128)}, /*index=5*/f32[35,64,256]...) while((s32[]{:T(128)}, f32[1024]{0:T(1024)S(1)}, ...), condition=%wide.region_14.15_spmd.clone.clone.clone, body=%wide.region_10.14_spmd.clone.clone.clone.sunk | while | flops 413276160 | bytes 354103 | solution.py:285
  1015.2 4.6 all-to-all-start.5
  1019.9 5.6 all_gather.6
  1027.7 13.7 %psum.7 = f32[3,512]{0,1:T(8,128)S(1)} all-reduce(f32[3,512]{0,1:T(8,128)S(1)} %bitcast.383), channel_id=1, replica_groups=mesh['grid'=8,'bead'=4] {'bead'}, use_global_device_ids=true, to_apply=%region_15.16 | all-reduce | flops 1536 | bytes 12288 | tf_op jit(solution)/shard_map/psum | solution.py:293
  1041.6 5.6 all_gather.7
  1050.1 19.1 %reduce-scatter.5.cloned.1.call-done = f32[3,8,512]{2,1,0:T(8,128)} async-done(((f32[3,32,512]{2,1,0:T(8,128)}), f32[3,8,512]{2,1,0:T(8,128)}) %reduce-scatter.5.cloned.1.call-update) | async-done | bytes 49168 | tf_op jit(solution)/shard_map/reduce_scatter | solution.py:311
  1069.2 22.8 %reduce-scatter.3.cloned.1.call-done = f32[3,8,512]{2,1,0:T(8,128)} async-done(((f32[3,32,512]{2,1,0:T(8,128)}), f32[3,8,512]{2,1,0:T(8,128)}) %reduce-scatter.3.cloned.1.call-update) | async-done | bytes 49168 | tf_op jit(solution)/shard_map/reduce_scatter | solution.py:310
  (525 shorter events, 441.9 us)
Async XLA Ops:
  12.4 9.9 copy-start.13
  15.0 13.9 %all-to-all-start = ((f32[4,8,128]{2,0,1:T(4,128)}), f32[4,8,128]{2,0,1:T(4,128)S(1)}, u32[]{:S(2)}, u32[]{:S(2)}) async-start(f32[4,8,128]{2,0,1:T(4,128)} %copy.99), calls=%async_computation | async-start | bytes 32768 | tf_op jit(solution)/shard_map/all_to_all | solution.py:206
  83.7 7.8 collective-permute-start
  84.5 7.2 collective-permute-start.1
  242.3 4.6 copy-start
  242.3 4.6 copy-start.8
  273.9 99.3 %all-to-all-start.2 = ((f32[8,1,131072]{2,1,0:T(1,128)}), f32[8,1,131072]{2,1,0:T(1,128)}, u32[]{:S(2)}, u32[]{:S(2)}) async-start(f32[8,1,131072]{2,1,0:T(1,128)} %reshape.458), calls=%async_computation.2 | async-start | bytes 8388608 | tf_op jit(solution)/shard_map/all_to_all | solution.py:252
  418.1 4.2 copy-start.1
  431.8 2.9 copy-start.6
  473.0 97.3 %all-to-all-start.3 = ((f32[8,1,131072]{2,1,0:T(1,128)}), f32[8,1,131072]{2,1,0:T(1,128)}, u32[]{:S(2)}, u32[]{:S(2)}) async-start(f32[8,1,131072]{2,1,0:T(1,128)} %reshape.460), calls=%async_computation.3 | async-start | bytes 8388608 | tf_op jit(solution)/shard_map/all_to_all | solution.py:261
  610.3 4.2 copy-start.2
  648.3 5.0 copy-start.9
  648.3 5.0 copy-start.56
  648.3 53.2 %all-to-all-start.4 = ((f32[4,1,262144]{2,1,0:T(1,128)}), f32[4,1,262144]{2,1,0:T(1,128)}, u32[]{:S(2)}, u32[]{:S(2)}) async-start(f32[4,1,262144]{2,1,0:T(1,128)} %reshape.462), calls=%async_computation.4 | async-start | bytes 8388608 | tf_op jit(solution)/shard_map/all_to_all | solution.py:263
  653.3 25.2 %copy-start.14 = (s32[512,1]{0,1:T(1,128)S(1)}, s32[512,1]{0,1:T(1,128)}, u32[]{:S(2)}) copy-start(s32[512,1]{0,1:T(1,128)} %copy-done.13) | copy-start | bytes 6148
  759.1 9.3 copy-start.12
  763.6 7.8 collective-permute-start.2
  765.1 7.6 collective-permute-start.3
  768.4 5.9 copy-start.15
  768.4 5.9 copy-start.16
  768.4 5.9 copy-start.17
  768.4 5.9 copy-start.18
  768.4 5.9 copy-start.19
  768.5 5.8 copy-start.20
  768.5 5.8 copy-start.21
  768.5 5.8 copy-start.22
  768.5 5.8 copy-start.24
  768.5 5.8 copy-start.26
  768.5 5.8 copy-start.28
  768.5 5.8 copy-start.30
  768.5 5.8 copy-start.32
  768.5 5.8 copy-start.34
  768.5 5.8 copy-start.36
  768.6 5.8 copy-start.38
  768.6 5.8 copy-start.40
  768.6 5.8 copy-start.42
  768.6 5.8 copy-start.44
  768.6 5.8 copy-start.46
  768.6 5.8 copy-start.48
  768.6 5.8 copy-start.50
  768.6 5.8 copy-start.52
  768.6 5.8 copy-start.54
  768.6 5.8 copy-start.58
  774.5 267.1 %copy-start.10 = (f32[3,8,512]{2,1,0:T(8,128)S(1)}, f32[3,8,512]{2,1,0:T(8,128)}, u32[]{:S(2)}) copy-start(f32[3,8,512]{2,1,0:T(8,128)} %param.19) | copy-start | bytes 147460
  1014.6 32.9 %copy-start.55 = (f32[3,8,512]{2,1,0:T(8,128)S(1)}, f32[3,8,512]{2,1,0:T(8,128)}, u32[]{:S(2)}) copy-start(f32[3,8,512]{2,1,0:T(8,128)} %param.20) | copy-start | bytes 147460
  1015.2 11.2 %all-to-all-start.5 = ((f32[3,8,128]{2,0,1:T(4,128)}), f32[3,8,128]{2,0,1:T(4,128)S(1)}, u32[]{:S(2)}, u32[]{:S(2)}) async-start(f32[3,8,128]{2,0,1:T(4,128)} %copy.121), calls=%async_computation.5 | async-start | bytes 32768 | tf_op jit(solution)/shard_map/all_to_all | solution.py:289
  1019.9 49.3 %reduce-scatter.5.cloned.1.call-start = ((), (), s32[]{:S(2)}) async-start(), calls=%async_computation.9 | async-start | bytes 245760 | tf_op jit(solution)/shard_map/reduce_scatter | solution.py:311
  1048.9 43.1 %reduce-scatter.3.cloned.1.call-start = ((), (), s32[]{:S(2)}) async-start(), calls=%async_computation.8 | async-start | bytes 245760 | tf_op jit(solution)/shard_map/reduce_scatter | solution.py:310
  (22 other events, 23.8 us)
Sparse Core Ops, SparseCore 0:
  1049.0 20.1 reduce-scatter.4
  1072.2 19.7 reduce-scatter.2
where the time goes:
time: 1110 us; the launch traced here: 1100 us
  matrix products  306 us (28%)
  local copies, waits for them, and re-layouts  283 us (25%)
  waiting for transfers between devices  262 us (24%)
  other arithmetic  105 us (9%)
  blocking collectives  78.7 us (7%)
  starting transfers between devices  38.2 us (3%)
  between operations  15.6 us (1%)
    dot_general x35, matrix products, gather_plane(): jnp.einsum('yz,yr->zr', layer_values, row_weight, precision=highest)  99 us
    all_to_all x1, waiting for transfers between devices, per_device(): lax.all_to_all(spectrum, 'grid', split_axis=1, concat_axis=2, tiled=True)  92.5 us
    all_to_all x1, waiting for transfers between devices, per_device(): lax.all_to_all(spectrum, 'grid', split_axis=2, concat_axis=1, tiled=True)  90.7 us
    dot_general x35, matrix products, gather_plane(): jnp.einsum('yz,yr->zr', layer_values, row_slope, precision=highest)  85.9 us
    unnamed x126, local copies, waits for them, and re-layouts  77.7 us
    all_to_all x1, blocking collectives, per_device(): lax.all_to_all(jnp.stack([real_part, imag_part]), 'bead', split_axis=3, c...  53.8 us
    dot_general x35, matrix products, spread_plane(): jnp.einsum('yr,zr->yz', weighted, depth_weight, precision=highest)  50.2 us
    unnamed x12, matrix products  39.9 us
  transfers between devices with their start and end apart: 11, of which 11 were waited for; matrix products, arithmetic and copies ran while one was open for 2% of the time, Pallas kernels for 0%

commit v1 on v0

v1 whole, which is shorter than its diff:
```python
import functools
import math

import jax
import jax.numpy as jnp
import numpy as np
from jax import lax
from jax.experimental import pallas as pl
from jax.experimental.pallas import tpu as pltpu
from jax.sharding import PartitionSpec as P

GX = 256
GY = 256
GZ = 256
BEADS = 32
TILE = 128
NBR = 4


highest = lax.Precision.HIGHEST
time_step = 0.5
polymer_frequency = 1.0
centroid_friction = 0.5
coulomb_scale = 100000.0
screen_width = 200.0
pair_strength = 1.0 / 128.0
pair_range = 4.0


def spline(fraction):
    remain = 1.0 - fraction
    square = fraction * fraction
    cubic = square * fraction
    values = [
        remain * remain * remain / 6.0,
        (3.0 * cubic - 6.0 * square + 4.0) / 6.0,
        (-3.0 * cubic + 3.0 * square + 3.0 * fraction + 1.0) / 6.0,
        cubic / 6.0,
    ]
    slopes = [
        -0.5 * remain * remain,
        0.5 * (3.0 * square - 4.0 * fraction),
        0.5 * (-3.0 * square + 2.0 * fraction + 1.0),
        0.5 * square,
    ]
    return (values, slopes)


def pair_force(centre, beside_all):
    separation = centre[:, :, :, None] - beside_all[:, :, None, :]
    distance_sq = jnp.sum(separation * separation, axis=0)
    weight = pair_strength * jnp.exp(-distance_sq / pair_range)
    return jnp.sum(weight[None] * separation, axis=3)


def domain_force(local_positions, neighbours):
    tile_count = neighbours.shape[0]
    bead_total = local_positions.shape[1]
    shaped = local_positions.reshape(3, bead_total, tile_count, TILE)

    def one_tile(tile_index):
        centre = lax.dynamic_index_in_dim(shaped, tile_index, 2, keepdims=False)
        beside_all = jnp.take(shaped, neighbours[tile_index], axis=2).reshape(
            3, bead_total, NBR * TILE
        )
        return pair_force(centre, beside_all)

    forces = lax.map(one_tile, jnp.arange(tile_count, dtype=jnp.int32))
    return jnp.moveaxis(forces, 0, 2).reshape(3, bead_total, tile_count * TILE)


def grid_positions(target, cells, offsets, planes):
    first = (target * planes + cells[0]).astype(jnp.float32) + offsets[0]
    second = cells[1].astype(jnp.float32) + offsets[1]
    third = cells[2].astype(jnp.float32) + offsets[2]
    return jnp.stack([first, second, third])


def real_waves(length):
    half = length // 2
    row = np.arange(length)
    wave = np.where(row <= half, row, row - half)
    angle = (wave[:, None] * np.arange(length)[None, :] % length) * (2.0 * math.pi / length)
    table = np.where((row <= half)[:, None], np.cos(angle), np.sin(angle))
    count = np.where((wave == 0) | (wave == half), 1.0, 2.0)
    return table, wave, count


def split_table(table):
    high = table.astype(jnp.bfloat16)
    low = (table - high.astype(np.float64)).astype(jnp.bfloat16)
    return high, low


def split(value):
    high = value.astype(jnp.bfloat16)
    low = (value - high.astype(jnp.float32)).astype(jnp.bfloat16)
    return high, low


def dot3(left, right, dims):
    def one(a, b):
        return lax.dot_general(a, b, (dims, ((), ())), preferred_element_type=jnp.float32)

    return one(left[0], right[0]) + (one(left[0], right[1]) + one(left[1], right[0]))


def stencil(position, length, with_slope):
    lowest = jnp.floor(position)
    values, slopes = spline(position - lowest)
    cell = lax.broadcasted_iota(jnp.int32, (length, position.shape[1]), 0)
    step = (cell - (lowest.astype(jnp.int32) - 1)) & (length - 1)
    hits = [step == offset for offset in range(4)]

    def dense(members):
        out = jnp.zeros(step.shape, jnp.float32)
        for offset in range(4):
            out = jnp.where(hits[offset], members[offset], out)
        return out

    return (dense(values), dense(slopes)) if with_slope else (dense(values),)


def mesh_kernel(chunks, group, fields, rxh, rxl, ryh, ryl, rzh, rzl, screen, out, total, gh, gl, xs, xd):
    step = pl.program_id(0)
    nx = rxh.shape[0]
    ny = ryh.shape[0]
    atoms = fields.shape[1]
    rows = group * ny
    nn = ((1,), (0,))
    nt = ((1,), (1,))

    def along(high, low, dense):
        return dot3((high[...], low[...]), split(dense), nn)

    @pl.when(step == 0)
    def _():
        total[...] = jnp.zeros_like(total)

    @pl.when(step < chunks)
    def _():
        xs[...] = along(rxh, rxl, stencil(fields[1:2, :], GX, False)[0]) * fields[0:1, :]
        ys = along(ryh, ryl, stencil(fields[2:3, :], GY, False)[0])
        zs = split(along(rzh, rzl, stencil(fields[3:4, :], GZ, False)[0]))

        def body(index, carry):
            parts = [xs[pl.ds(index * group + j, 1), :] * ys for j in range(group)]
            pair = split(jnp.concatenate(parts, axis=0))
            where = pl.ds(pl.multiple_of(index * rows, rows), rows)
            total[where, :] += dot3(pair, zs, nt)
            return carry

        lax.fori_loop(0, nx // group, body, 0)

    @pl.when(step == chunks - 1)
    def _():
        def body(index, carry):
            where = pl.ds(pl.multiple_of(index * rows, rows), rows)
            high, low = split(total[where, :] * screen[where, :])
            gh[where, :] = high
            gl[where, :] = low
            return carry

        lax.fori_loop(0, nx // group, body, 0)

    @pl.when(step >= chunks)
    def _():
        value, slope = stencil(fields[1:2, :], GX, True)
        xs[...] = along(rxh, rxl, value)
        xd[...] = along(rxh, rxl, slope)
        value, slope = stencil(fields[2:3, :], GY, True)
        ys = along(ryh, ryl, value)
        yd = along(ryh, ryl, slope)
        value, slope = stencil(fields[3:4, :], GZ, True)
        zs = split(along(rzh, rzl, value))
        zd = split(along(rzh, rzl, slope))

        def body(index, carry):
            force_x, force_y, force_z = carry
            where = pl.ds(pl.multiple_of(index * rows, rows), rows)
            filtered = (gh[where, :], gl[where, :])
            plain = dot3(filtered, zs, nn)
            steep = dot3(filtered, zd, nn)
            for j in range(group):
                own = plain[j * ny : (j + 1) * ny]
                x_here = xs[pl.ds(index * group + j, 1), :]
                force_x += xd[pl.ds(index * group + j, 1), :] * jnp.sum(own * ys, axis=0, keepdims=True)
                force_y += x_here * jnp.sum(own * yd, axis=0, keepdims=True)
                force_z += x_here * jnp.sum(
                    steep[j * ny : (j + 1) * ny] * ys, axis=0, keepdims=True
                )
            return force_x, force_y, force_z

        empty = jnp.zeros((1, atoms), jnp.float32)
        found = lax.fori_loop(0, nx // group, body, (empty, empty, empty))
        for c in range(3):
            out[c : c + 1, :] = -fields[0:1, :] * found[c]


def mesh_forces(fields, row_x, row_y, nx, ny):
    table_x, wave_x, count_x = real_waves(GX)
    table_y, wave_y, count_y = real_waves(GY)
    table_z, wave_z, count_z = real_waves(GZ)

    def rows_of(values, first, count):
        return lax.dynamic_slice_in_dim(jnp.asarray(values), first, count, 0)

    own = [rows_of(part, row_x, nx) for part in split_table(table_x)]
    own += [rows_of(part, row_y, ny) for part in split_table(table_y)]
    own += [jnp.asarray(part) for part in split_table(table_z)]
    square_x = rows_of((wave_x**2).astype(np.float32), row_x, nx)
    square_y = rows_of((wave_y**2).astype(np.float32), row_y, ny)
    times_x = rows_of((count_x / float(GX)).astype(np.float32), row_x, nx)
    times_y = rows_of((count_y / float(GY)).astype(np.float32), row_y, ny)
    square_z = jnp.asarray((wave_z**2).astype(np.float32))
    times_z = jnp.asarray((count_z / float(GZ)).astype(np.float32))
    square = (square_x[:, None] + square_y[None, :]).reshape(nx * ny, 1) + square_z[None, :]
    times = (times_x[:, None] * times_y[None, :]).reshape(nx * ny, 1) * times_z[None, :]
    centre = square == 0.0
    screen = jnp.where(
        centre,
        0.0,
        coulomb_scale
        * jnp.exp(-square / (2.0 * screen_width * screen_width))
        / jnp.where(centre, 1.0, square),
    )
    screen = screen * times

    atoms = fields.shape[1]
    width = min(512, atoms)
    chunks = atoms // width
    group = min(8, nx)
    full = lambda array: pl.BlockSpec(array.shape, lambda s: (0, 0))
    operands = [fields, *own, screen]
    return pl.pallas_call(
        functools.partial(mesh_kernel, chunks, group),
        grid=(2 * chunks,),
        out_shape=jax.ShapeDtypeStruct((3, atoms), jnp.float32),
        in_specs=[pl.BlockSpec((4, width), lambda s: (0, s % chunks))]
        + [full(array) for array in operands[1:]],
        out_specs=pl.BlockSpec((3, width), lambda s: (0, jnp.maximum(s - chunks, 0))),
        scratch_shapes=[
            pltpu.VMEM((nx * ny, GZ), jnp.float32),
            pltpu.VMEM((nx * ny, GZ), jnp.bfloat16),
            pltpu.VMEM((nx * ny, GZ), jnp.bfloat16),
            pltpu.VMEM((nx, width), jnp.float32),
            pltpu.VMEM((nx, width), jnp.float32),
        ],
        compiler_params=pltpu.CompilerParams(
            dimension_semantics=("arbitrary",), vmem_limit_bytes=48 * 1024 * 1024
        ),
        cost_estimate=pl.CostEstimate(
            flops=18 * nx * ny * GZ * atoms, bytes_accessed=8 * nx * ny * GZ, transcendentals=0
        ),
    )(*operands)


def step_tables(bead_total):
    mode = np.arange(bead_total)
    angle = (mode[:, None] * mode[None, :] % bead_total) * (2.0 * math.pi / bead_total)
    middle = bead_total // 2
    scaled = math.sqrt(2.0 / bead_total)
    column = mode[:, None]
    matrix = np.where(
        column == 0,
        1.0 / math.sqrt(bead_total),
        np.where(
            column < middle,
            scaled * np.cos(angle),
            np.where(
                column == middle, np.cos(angle) / math.sqrt(bead_total), scaled * np.sin(angle)
            ),
        ),
    )
    half = 0.5 * time_step
    frequency = 2.0 * polymer_frequency * np.sin(mode * (math.pi / bead_total))
    cosine = np.cos(frequency * half)
    drift = np.where(mode == 0, half, np.sin(frequency * half) / np.where(mode == 0, 1.0, frequency))
    pull = frequency * np.sin(frequency * half)
    friction = np.where(mode == 0, centroid_friction, 2.0 * frequency)
    damping = np.exp(-friction * time_step)
    kick = np.sqrt(1.0 - damping * damping)
    factors = [
        [cosine * cosine - drift * damping * pull, drift * cosine * (1.0 + damping), drift * kick],
        [-cosine * pull * (1.0 + damping), cosine * damping * cosine - pull * drift, cosine * kick],
    ]
    tables = np.stack(
        [
            np.stack(
                [
                    matrix.T @ (row[0][:, None] * matrix),
                    matrix.T @ (row[1][:, None] * matrix),
                    matrix.T * row[2][None, :],
                ]
            )
            for row in factors
        ]
    )
    return tables.astype(np.float32), (float(factors[0][1][0]), float(factors[1][1][0]))


def per_device(positions, momenta, noise, charges, slab_route, cells, offsets, nbr_tiles):
    grid_count = lax.axis_size("grid")
    bead_count = lax.axis_size("bead")
    grid_rank = lax.axis_index("grid")
    bead_rank = lax.axis_index("bead")
    beads_local = positions.shape[1]
    nx = GX // grid_count
    ny = GY // bead_count
    half_step = 0.5 * time_step

    grid_pos = grid_positions(slab_route[:, 0], cells, offsets, nx)
    fields = jnp.concatenate([charges[None, :], grid_pos], axis=0)
    fields = lax.all_gather(fields, "grid", axis=1, tiled=True)
    partial = mesh_forces(fields, grid_rank * nx, bead_rank * ny, nx, ny)
    mesh_force = lax.psum_scatter(partial, "grid", scatter_dimension=1, tiled=True)
    mesh_force = half_step * lax.psum(mesh_force, "bead")

    kicked = momenta + half_step * domain_force(positions, nbr_tiles)
    sources = lax.all_gather(
        jnp.stack([positions, kicked, noise]), "bead", axis=2, tiled=True
    )
    tables, (centre_q, centre_p) = step_tables(beads_local * bead_count)
    own = lax.dynamic_slice_in_dim(jnp.asarray(tables), bead_rank * beads_local, beads_local, 2)
    stepped = jnp.einsum("okbm,kcma->ocba", own, sources, precision=highest)
    return (
        stepped[0] + centre_q * mesh_force[:, None, :],
        stepped[1] + centre_p * mesh_force[:, None, :],
    )


def solution(mesh):
    in_specs = (
        P(None, "bead", "grid"),
        P(None, "bead", "grid"),
        P(None, "bead", "grid"),
        P("grid"),
        P("grid", None),
        P(None, "grid"),
        P(None, "grid"),
        P("grid", None),
    )
    out_specs = (P(None, "bead", "grid"), P(None, "bead", "grid"))
    return jax.shard_map(
        per_device, mesh=mesh, in_specs=in_specs, out_specs=out_specs, check_vma=False
    )
```

time: 1110 us -> 211 us (0.19)
  matrix products: 306 us -> 1.16 us
  local copies, waits for them, and re-layouts: 283 us -> 12.7 us
  waiting for transfers between devices: 262 us -> 36.4 us
  other arithmetic: 105 us -> 15.2 us
  Pallas kernels: 0 us -> 76.8 us
  starting transfers between devices: 38.2 us -> 0.04 us
  blocking collectives: 78.7 us -> 45.6 us
    dot_general x117 -> x1, matrix products: 267 us -> 1.16 us  [per_device(): stepped = jnp.einsum('okbm,kcma->ocba', own, sources, precision=highest)]
    all_to_all x5 -> x0, waiting for transfers between devices: 213 us -> none  [the longest x1 92.5 us: per_device(): lax.all_to_all(spectrum, 'grid', split_axis=1, concat_axis=2, tiled=True)]
    pallas_call x0 -> x1, Pallas kernels: none -> 76.8 us  [mesh_forces(): pl.pallas_call(functools.partial(mesh_kernel, chunks, group), grid=(2 * c...]
    unnamed x126 -> x14, local copies, waits for them, and re-layouts: 77.7 us -> 3.08 us
    all_to_all x4 -> x0, other arithmetic: 70.5 us -> none  [the longest x1 27.1 us: per_device(): lax.all_to_all(jnp.stack([real_part, imag_part]), 'bead', split_axis=3, c...]
    all_to_all x1 -> x0, blocking collectives: 53.8 us -> none  [per_device(): lax.all_to_all(jnp.stack([real_part, imag_part]), 'bead', split_axis=3, c...]
    dynamic_slice x108 -> x6, local copies, waits for them, and re-layouts: 54.3 us -> 4.57 us  [rows_of(): return lax.dynamic_slice_in_dim(jnp.asarray(values), first, count, 0)]
    reduce_scatter x2 -> x0, waiting for transfers between devices: 41.9 us -> none  [the longest x1 22.8 us: per_device(): lax.psum_scatter(share_q, 'bead', scatter_dimension=1, tiled=True)]
  transfers between devices with their start and end apart: 11 -> 1, of which waited for: 11 -> 1; matrix products, arithmetic and copies ran while one was open for 2% -> 8% of each run, Pallas kernels for 0% -> 0%
where the time goes in v1:
time: 211 us; the launch traced here: 210 us
  Pallas kernels  76.8 us (36%)
  blocking collectives  45.6 us (22%)
  waiting for transfers between devices  36.4 us (17%)
  other arithmetic  15.2 us (7%)
  between operations  14.2 us (7%)
  local copies, waits for them, and re-layouts  12.7 us (6%)
  loops' own time  8.09 us (4%)
    pallas_call x1, Pallas kernels, mesh_forces(): pl.pallas_call(functools.partial(mesh_kernel, chunks, group), grid=(2 * c...  76.8 us
    unnamed x2, waiting for transfers between devices  36.4 us
    all_gather x1, blocking collectives, per_device(): fields = lax.all_gather(fields, 'grid', axis=1, tiled=True)  32.4 us
    another operation x1, loops' own time, domain_force(): forces = lax.map(one_tile, jnp.arange(tile_count, dtype=jnp.int32))  8.09 us
    all_gather x1, blocking collectives, per_device(): lax.all_gather(jnp.stack([positions, kicked, noise]), 'bead', axis=2, til...  7.53 us
    psum x1, blocking collectives, per_device(): mesh_force = half_step * lax.psum(mesh_force, 'bead')  5.75 us
    reduce_sum x4, other arithmetic, pair_force(): return jnp.sum(weight[None] * separation, axis=3)  5.45 us
    dynamic_slice x6, local copies, waits for them, and re-layouts, rows_of(): return lax.dynamic_slice_in_dim(jnp.asarray(values), first, count, 0)  4.57 us
  transfers between devices with their start and end apart: 1, of which 1 were waited for; matrix products, arithmetic and copies ran while one was open for 8% of the time, Pallas kernels for 0%

profile of v1, /device:TPU:0, one launch (start us, length us, event | category | flops | bytes accessed | tf_op | source)
XLA Modules:
  0.0 210.2 jit_solution(18126730941062153787)
XLA Ops:
  7.2 0.0 reduce-scatter.4.cloned.1.call-start
  7.2 0.8 dynamic_slice.44
  8.0 0.8 dynamic_slice.43
  8.8 0.8 dynamic_slice.46
  9.5 0.8 dynamic_slice.45
  10.3 0.8 constant_dynamic-slice_fusion.1
  11.1 0.7 constant_dynamic-slice_fusion.3
  11.8 0.1 broadcast_add_fusion
  11.9 0.1 add.121
  12.0 0.1 broadcast_multiply_fusion
  12.0 0.1 mul.128
  12.1 0.8 fusion.16
  12.9 0.7 pad_maximum_fusion.1
  13.6 32.4 %all_gather.7.fields = f32[4,4096]{1,0:T(4,128)S(1)} all-gather(f32[4,512]{1,0:T(4,128)S(1)} %pad_maximum_fusion.1), channel_id=1, replica_groups=mesh['grid'=8,'bead'=4] {'grid'}, dimensions={1}, use_global_device_ids=true | all-gather | bytes 73728 | tf_op jit(solution)/shard_map/all_gather | solution.py:314
  46.0 1.6 fusion.4.screen
  47.6 76.8 %shard_map.212 = f32[3,4096]{1,0:T(4,128)S(1)} custom-call(f32[4,4096]{1,0:T(4,128)S(1)} %all_gather.7.fields, bf16[32,256]{1,0:T(8,128)(2,1)S(1)} %get-tuple-element.48.rxh, bf16[32,256]{1,0:T(8,128)(2,1)S(1)} %get-tuple-element.47.rxl, bf16[64,256]{1,0:T(8,128)(2,1)S(1)} %get-tuple-element.50.ryh, bf16[64,256]{1,0:T(8,128)(2,1)S(1)} %get-tuple-element.49.ryl, ...), custom_call_target="tpu_custom_call" | custom-call | flops 38654705664 | bytes 4194304 | tf_op jit(solution)/shard_map/pallas_call | solution.py:235
  124.5 2.0 copy.33
  126.6 24.3 %while.10 = (s32[]{:T(128)}, f32[4,3,8,128]{3,2,1,0:T(8,128)S(1)}, s32[4]{0:T(128)S(1)}, f32[3,8,4,128]{3,1,2,0:T(8,128)S(1)}, s32[4,4]{1,0:T(4,128)S(1)}, /*index=5*/s32[]{:T(128)}, s32[]{:T(128)}, s32[]{:T(128)}) while((s32[]{:T(128)}, f32[4,3,8,128]{3,2,1,0:T(8,128)S(1)}, s32[4]{0:T(128)S(1)}, f32[3,8,4,128]{3,1,2,0:T(8,128)S(1)}, ...), condition=%wide.region_3.4_spmd, body=%wide.region_0.3_spmd.sunk | while | flops 10496041 | bytes 8774891 | solution.py:68
  126.6 0.6 dynamic_slice.68
  129.1 0.6 gather_fusion
  129.7 0.1 broadcast_bitcast_fusion.2
  129.8 1.0 fusion.25
  130.8 0.4 exponential_multiply_fusion.2
  131.2 1.4 fusion.26
  132.6 0.6 dynamic_slice.68
  135.2 0.6 gather_fusion
  135.8 0.1 broadcast_bitcast_fusion.2
  135.9 1.0 fusion.25
  136.9 0.4 exponential_multiply_fusion.2
  137.3 1.4 fusion.26
  138.7 0.6 dynamic_slice.68
  141.3 0.6 gather_fusion
  141.8 0.1 broadcast_bitcast_fusion.2
  141.9 1.0 fusion.25
  142.9 0.4 exponential_multiply_fusion.2
  143.4 1.4 fusion.26
  144.8 0.6 dynamic_slice.68
  147.3 0.6 gather_fusion
  147.9 0.1 broadcast_bitcast_fusion.2
  148.0 1.0 fusion.25
  149.0 0.4 exponential_multiply_fusion.2
  149.4 1.4 fusion.26
  150.9 7.5 %all_gather.6 = f32[3,3,32,512]{3,2,0,1:T(8,128)S(1)} all-gather(f32[3,3,8,512]{3,2,0,1:T(8,128)S(1)} %pad_maximum_fusion), channel_id=1, replica_groups=mesh['grid'=8,'bead'=4] {'bead'}, dimensions={2}, use_global_device_ids=true | all-gather | bytes 737280 | tf_op jit(solution)/shard_map/all_gather | solution.py:320
  158.4 1.2 convolution_bitcast_fusion
  159.6 36.4 %reduce-scatter.4.cloned.1.call-done = f32[512,3]{1,0:T(8,128)} async-done(((f32[4096,3]{1,0:T(8,128)}), f32[512,3]{1,0:T(8,128)}) %reduce-scatter.4.cloned.1.call-update) | async-done | bytes 6160
  195.9 1.1 copy.34
  197.0 5.7 %psum.7 = f32[3,512]{1,0:T(4,128)S(1)} all-reduce(f32[3,512]{1,0:T(4,128)S(1)} %copy.34), channel_id=1, replica_groups=mesh['grid'=8,'bead'=4] {'bead'}, use_global_device_ids=true, to_apply=%region_5.6 | all-reduce | flops 1536 | bytes 12288 | tf_op jit(solution)/shard_map/psum | solution.py:317
  202.8 0.6 fusion.10
  (42 shorter events, 0.3 us)
Async XLA Ops:
  7.2 40.4 %copy-start = (bf16[256,256]{1,0:T(8,128)(2,1)S(1)}, bf16[256,256]{1,0:T(8,128)(2,1)}, u32[]{:S(2)}) copy-start(bf16[256,256]{1,0:T(8,128)(2,1)} %constant.85.clone.rzh) | copy-start | bytes 393220
  7.2 40.4 %copy-start.1 = (bf16[256,256]{1,0:T(8,128)(2,1)S(1)}, bf16[256,256]{1,0:T(8,128)(2,1)}, u32[]{:S(2)}) copy-start(bf16[256,256]{1,0:T(8,128)(2,1)} %constant.86.clone.rzl) | copy-start | bytes 393220
  7.2 188.7 %reduce-scatter.4.cloned.1.call-start = ((), (), s32[]{:S(2)}) async-start(), calls=%async_computation.1 | async-start | bytes 2359296
  124.5 2.1 copy-start.2
  124.5 2.1 copy-start.5
  126.5 24.3 %copy-start.4 = (f32[3,8,512]{2,1,0:T(8,128)S(1)}, f32[3,8,512]{2,1,0:T(8,128)}, u32[]{:S(2)}) copy-start(f32[3,8,512]{2,1,0:T(8,128)} %param.24) | copy-start | bytes 147460
  126.5 24.3 %copy-start.3 = (f32[3,8,512]{2,1,0:T(8,128)S(1)}, f32[3,8,512]{2,1,0:T(8,128)}, u32[]{:S(2)}) copy-start(f32[3,8,512]{2,1,0:T(8,128)} %param.25) | copy-start | bytes 147460
Sparse Core Ops, SparseCore 0:
  126.6 69.2 reduce-scatter.3

commit v2 on v1

--- a/solution.py
+++ b/solution.py
@@ -46,27 +46,48 @@
     return (values, slopes)
 
 
-def pair_force(centre, beside_all):
-    separation = centre[:, :, :, None] - beside_all[:, :, None, :]
-    distance_sq = jnp.sum(separation * separation, axis=0)
-    weight = pair_strength * jnp.exp(-distance_sq / pair_range)
-    return jnp.sum(weight[None] * separation, axis=3)
-
-
-def domain_force(local_positions, neighbours):
-    tile_count = neighbours.shape[0]
-    bead_total = local_positions.shape[1]
-    shaped = local_positions.reshape(3, bead_total, tile_count, TILE)
-
-    def one_tile(tile_index):
-        centre = lax.dynamic_index_in_dim(shaped, tile_index, 2, keepdims=False)
-        beside_all = jnp.take(shaped, neighbours[tile_index], axis=2).reshape(
-            3, bead_total, NBR * TILE
-        )
-        return pair_force(centre, beside_all)
-
-    forces = lax.map(one_tile, jnp.arange(tile_count, dtype=jnp.int32))
-    return jnp.moveaxis(forces, 0, 2).reshape(3, bead_total, tile_count * TILE)
+def pair_kernel(counts, places, momenta, kicked):
+    beads, atoms = places.shape[1:]
+    tiles = atoms // TILE
+    across = [places[c].T for c in range(3)]
+
+    def body(t, carry):
+        where = pl.ds(pl.multiple_of(t * TILE, TILE), TILE)
+        for b in range(beads):
+            centre = [places[c, b : b + 1, where] for c in range(3)]
+            sums = [jnp.zeros((8, TILE), jnp.float32) for _ in range(3)]
+            for m in range(tiles):
+                apart = [
+                    centre[c] - across[c][m * TILE : (m + 1) * TILE, b : b + 1] for c in range(3)
+                ]
+                square = apart[0] * apart[0] + apart[1] * apart[1] + apart[2] * apart[2]
+                weight = jnp.exp(square * (-1.0 / pair_range))
+                for c in range(3):
+                    part = jnp.sum((weight * apart[c]).reshape(TILE // 8, 8, TILE), axis=0)
+                    sums[c] = sums[c] + counts[t, m] * part
+            for c in range(3):
+                force = jnp.sum(sums[c], axis=0, keepdims=True)
+                kicked[c, b : b + 1, where] = momenta[c, b : b + 1, where] + force
+        return carry
+
+    lax.fori_loop(0, tiles, body, 0)
+
+
+def kick_short(positions, momenta, neighbours):
+    tiles = neighbours.shape[0]
+    listed = neighbours[:, :, None] == jnp.arange(tiles, dtype=jnp.int32)
+    counts = jnp.sum(listed.astype(jnp.float32), axis=1) * (0.5 * time_step * pair_strength)
+    pairs = positions.shape[1] * positions.shape[2] ** 2
+    vmem = pl.BlockSpec(memory_space=pltpu.VMEM)
+    return pl.pallas_call(
+        pair_kernel,
+        out_shape=jax.ShapeDtypeStruct(momenta.shape, jnp.float32),
+        in_specs=[pl.BlockSpec(memory_space=pltpu.SMEM), vmem, vmem],
+        out_specs=vmem,
+        cost_estimate=pl.CostEstimate(
+            flops=20 * pairs, bytes_accessed=12 * positions.size, transcendentals=pairs
+        ),
+    )(counts, positions, momenta)
 
 
 def grid_positions(target, cells, offsets, planes):
@@ -311,12 +332,16 @@
 
     grid_pos = grid_positions(slab_route[:, 0], cells, offsets, nx)
     fields = jnp.concatenate([charges[None, :], grid_pos], axis=0)
-    fields = lax.all_gather(fields, "grid", axis=1, tiled=True)
+    copies = jnp.broadcast_to(fields[:, None, :], (4, grid_count, charges.shape[0]))
+    fields = lax.all_to_all(copies, "grid", split_axis=1, concat_axis=1, tiled=True)
+    fields = fields.reshape(4, grid_count * charges.shape[0])
     partial = mesh_forces(fields, grid_rank * nx, bead_rank * ny, nx, ny)
-    mesh_force = lax.psum_scatter(partial, "grid", scatter_dimension=1, tiled=True)
-    mesh_force = half_step * lax.psum(mesh_force, "bead")
-
-    kicked = momenta + half_step * domain_force(positions, nbr_tiles)
+    shares = lax.all_to_all(
+        partial.reshape(3, grid_count, charges.shape[0]), "grid", split_axis=1, concat_axis=1, tiled=True
+    )
+    mesh_force = half_step * lax.psum(jnp.sum(shares, axis=1), "bead")
+
+    kicked = kick_short(positions, momenta, nbr_tiles)
     sources = lax.all_gather(
         jnp.stack([positions, kicked, noise]), "bead", axis=2, tiled=True
     )

time: 211 us -> 131 us (0.62)
  blocking collectives: 45.6 us -> 13.7 us
  waiting for transfers between devices: 36.4 us -> 5.74 us
  between operations: 14.2 us -> 0.73 us
  starting transfers between devices: 0.04 us -> 13.5 us
  other arithmetic: 15.2 us -> 5.44 us
  Pallas kernels: 76.8 us -> 86.2 us
  local copies, waits for them, and re-layouts: 12.7 us -> 3.84 us
  loops' own time: 8.09 us -> 0 us
    unnamed x2 -> x0, waiting for transfers between devices: 36.4 us -> none
    all_gather x1 -> x0, blocking collectives: 32.4 us -> none  [per_device(): fields = lax.all_gather(fields, 'grid', axis=1, tiled=True)]
    all_to_all x0 -> x2, starting transfers between devices: none -> 13.5 us  [the longest x1 7.44 us: per_device(): lax.all_to_all(copies, 'grid', split_axis=1, concat_axis=1, tiled=True)]
    pallas_call x0 -> x1, Pallas kernels: none -> 8.67 us  [kick_short(): pl.pallas_call(pair_kernel, out_shape=jax.ShapeDtypeStruct(momenta.shape,...]
    reduce_sum x8 -> x2, other arithmetic: 9.45 us -> 0.8 us  [the longest x1 0.77 us: kick_short(): jnp.sum(listed.astype(jnp.float32), axis=1)]
    another operation x1 -> x0, loops' own time: 8.09 us -> none  [domain_force(): forces = lax.map(one_tile, jnp.arange(tile_count, dtype=jnp.int32))]
    all_to_all x0 -> x2, waiting for transfers between devices: none -> 5.74 us  [the longest x1 5.74 us: per_device(): lax.all_to_all(partial.reshape(3, grid_count, charges.shape[0]), 'grid',...]
    unnamed x14 -> x12, local copies, waits for them, and re-layouts: 3.08 us -> 0.02 us
  transfers between devices with their start and end apart: 1 -> 2, of which waited for: 1 -> 1; matrix products, arithmetic and copies ran while one was open for 8% -> 6% of each run, Pallas kernels for 0% -> 7%
where the time goes in v2:
time: 131 us; the launch traced here: 130 us
  Pallas kernels  86.2 us (66%)
  blocking collectives  13.7 us (10%)
  starting transfers between devices  13.5 us (10%)
  waiting for transfers between devices  5.74 us (4%)
  other arithmetic  5.44 us (4%)
  local copies, waits for them, and re-layouts  3.84 us (3%)
    pallas_call x1, Pallas kernels, mesh_forces(): pl.pallas_call(functools.partial(mesh_kernel, chunks, group), grid=(2 * c...  77.6 us
    pallas_call x1, Pallas kernels, kick_short(): pl.pallas_call(pair_kernel, out_shape=jax.ShapeDtypeStruct(momenta.shape,...  8.67 us
    all_gather x1, blocking collectives, per_device(): lax.all_gather(jnp.stack([positions, kicked, noise]), 'bead', axis=2, til...  7.53 us
    all_to_all x1, starting transfers between devices, per_device(): lax.all_to_all(copies, 'grid', split_axis=1, concat_axis=1, tiled=True)  7.44 us
    psum x1, blocking collectives, per_device(): mesh_force = half_step * lax.psum(jnp.sum(shares, axis=1), 'bead')  6.14 us
    all_to_all x1, starting transfers between devices, per_device(): lax.all_to_all(partial.reshape(3, grid_count, charges.shape[0]), 'grid',...  6.06 us
    all_to_all x1, waiting for transfers between devices, per_device(): lax.all_to_all(partial.reshape(3, grid_count, charges.shape[0]), 'grid',...  5.74 us
    dynamic_slice x6, local copies, waits for them, and re-layouts, rows_of(): return lax.dynamic_slice_in_dim(jnp.asarray(values), first, count, 0)  3.03 us
  transfers between devices with their start and end apart: 2, of which 1 were waited for; matrix products, arithmetic and copies ran while one was open for 6% of the time, Pallas kernels for 7%

profile of v2, /device:TPU:0, one launch (start us, length us, event | category | flops | bytes accessed | tf_op | source)
XLA Modules:
  0.0 130.3 jit_solution(4498489944595158639)
XLA Ops:
  0.6 0.8 fusion.12
  1.5 0.7 pad_maximum_fusion.1
  2.2 0.6 broadcast_in_dim.9
  2.8 0.0 copy-start.2
  2.8 0.0 copy-start.3
  2.8 7.4 %all-to-all-start = ((f32[4,8,512]{2,0,1:T(4,128)}), f32[4,8,512]{2,0,1:T(4,128)S(1)}, u32[]{:S(2)}, u32[]{:S(2)}) async-start(f32[4,8,512]{2,0,1:T(4,128)} %broadcast_in_dim.9), calls=%async_computation | async-start | bytes 131072 | tf_op jit(solution)/shard_map/all_to_all | solution.py:336
  10.2 0.8 dynamic_slice.33
  11.0 0.8 dynamic_slice.32
  11.8 0.8 dynamic_slice.35
  12.5 0.8 dynamic_slice.34
  13.3 0.1 broadcast_add_fusion
  13.3 0.1 add.92
  13.4 0.1 broadcast_multiply_fusion
  13.5 0.1 mul.98
  13.5 0.8 convert_reduce_fusion
  14.3 0.6 broadcast_multiply_fusion.3.counts
  14.9 0.0 copy-start.4
  14.9 0.0 copy-start.5
  14.9 8.7 %shard_map.212 = f32[3,8,512]{2,1,0:T(8,128)} custom-call(f32[4,4]{1,0:T(4,128)} %broadcast_multiply_fusion.3.counts, f32[3,8,512]{2,1,0:T(8,128)} %places.1, f32[3,8,512]{2,1,0:T(8,128)} %momenta.1), custom_call_target="tpu_custom_call" | custom-call | flops 41943040 | bytes 147456 | tf_op jit(solution)/shard_map/pallas_call | solution.py:82
  23.6 0.0 copy-start
  23.6 0.0 copy-start.1
  23.6 0.0 copy-done.2
  23.6 0.0 copy-done.3
  23.6 0.9 pad_maximum_fusion
  24.4 7.5 %all_gather.3 = f32[3,3,32,512]{3,2,1,0:T(8,128)S(1)} all-gather(f32[3,3,8,512]{3,2,1,0:T(8,128)S(1)} %pad_maximum_fusion), channel_id=1, replica_groups=mesh['grid'=8,'bead'=4] {'bead'}, dimensions={2}, use_global_device_ids=true | all-gather | bytes 737280 | tf_op jit(solution)/shard_map/all_gather | solution.py:345
  32.0 0.0 copy-done.4
  32.0 0.0 copy-done.5
  32.0 0.9 fusion.1.screen
  32.9 0.0 copy-done
  32.9 0.0 copy-done.1
  32.9 0.0 all-to-all-done
  33.0 77.6 %shard_map.213 = f32[3,4096]{1,0:T(4,128)} custom-call(f32[4,4096]{1,0:T(4,128)S(1)} %bitcast.32, bf16[32,256]{1,0:T(8,128)(2,1)S(1)} %get-tuple-element.10.rxh, bf16[32,256]{1,0:T(8,128)(2,1)S(1)} %get-tuple-element.9.rxl, bf16[64,256]{1,0:T(8,128)(2,1)S(1)} %get-tuple-element.12.ryh, bf16[64,256]{1,0:T(8,128)(2,1)S(1)} %get-tuple-element.11.ryl, ...), custom_call_target="tpu_custom_call" | custom-call | flops 38654705664 | bytes 4194304 | tf_op jit(solution)/shard_map/pallas_call | solution.py:256
  110.5 6.1 %all-to-all-start.1 = ((f32[3,8,512]{2,0,1:T(4,128)}), f32[3,8,512]{2,0,1:T(4,128)S(1)}, u32[]{:S(2)}, u32[]{:S(2)}) async-start(f32[3,8,512]{2,0,1:T(4,128)} %bitcast.12), calls=%async_computation.1 | async-start | bytes 131072 | tf_op jit(solution)/shard_map/all_to_all | solution.py:339
  116.6 1.2 convolution_bitcast_fusion
  117.7 5.7 %all-to-all-done.1 = f32[3,8,512]{2,0,1:T(4,128)S(1)} async-done(((f32[3,8,512]{2,0,1:T(4,128)}), f32[3,8,512]{2,0,1:T(4,128)S(1)}, u32[]{:S(2)}, u32[]{:S(2)}) %all-to-all-start.1) | async-done | bytes 49184 | tf_op jit(solution)/shard_map/all_to_all | solution.py:339
  123.5 6.1 %psum.7 = f32[3,512]{1,0:T(4,128)S(1)} all-reduce(f32[3,512]{1,0:T(4,128)S(1)} %reduce_sum.19), channel_id=1, replica_groups=mesh['grid'=8,'bead'=4] {'bead'}, use_global_device_ids=true, to_apply=%region_2.3 | all-reduce | flops 1536 | bytes 12288 | tf_op jit(solution)/shard_map/psum | solution.py:342
  129.7 0.6 fusion.7
  (4 shorter events, 0.1 us)
Async XLA Ops:
  2.8 20.8 %copy-start.2 = (f32[3,8,512]{2,1,0:T(8,128)S(1)}, f32[3,8,512]{2,1,0:T(8,128)}, u32[]{:S(2)}) copy-start(f32[3,8,512]{2,1,0:T(8,128)} %param.23) | copy-start | bytes 147460
  2.8 20.8 %copy-start.3 = (f32[3,8,512]{2,1,0:T(8,128)S(1)}, f32[3,8,512]{2,1,0:T(8,128)}, u32[]{:S(2)}) copy-start(f32[3,8,512]{2,1,0:T(8,128)} %places.1) | copy-start | bytes 147460
  2.8 30.1 %all-to-all-start = ((f32[4,8,512]{2,0,1:T(4,128)}), f32[4,8,512]{2,0,1:T(4,128)S(1)}, u32[]{:S(2)}, u32[]{:S(2)}) async-start(f32[4,8,512]{2,0,1:T(4,128)} %broadcast_in_dim.9), calls=%async_computation | async-start | bytes 131072 | tf_op jit(solution)/shard_map/all_to_all | solution.py:336
  14.9 17.1 %copy-start.4 = (f32[256]{0:T(256)S(1)}, f32[256]{0:T(256)}, u32[]{:S(2)}) copy-start(f32[256]{0:T(256)} %constant.51.clone) | copy-start | bytes 3076
  14.9 17.1 %copy-start.5 = (f32[256]{0:T(256)S(1)}, f32[256]{0:T(256)}, u32[]{:S(2)}) copy-start(f32[256]{0:T(256)} %constant.52.clone) | copy-start | bytes 3076
  23.6 9.3 %copy-start = (bf16[256,256]{1,0:T(8,128)(2,1)S(1)}, bf16[256,256]{1,0:T(8,128)(2,1)}, u32[]{:S(2)}) copy-start(bf16[256,256]{1,0:T(8,128)(2,1)} %constant.49.clone.rzh) | copy-start | bytes 393220
  23.6 9.3 %copy-start.1 = (bf16[256,256]{1,0:T(8,128)(2,1)S(1)}, bf16[256,256]{1,0:T(8,128)(2,1)}, u32[]{:S(2)}) copy-start(bf16[256,256]{1,0:T(8,128)(2,1)} %constant.50.clone.rzl) | copy-start | bytes 393220
  110.5 13.0 %all-to-all-start.1 = ((f32[3,8,512]{2,0,1:T(4,128)}), f32[3,8,512]{2,0,1:T(4,128)S(1)}, u32[]{:S(2)}, u32[]{:S(2)}) async-start(f32[3,8,512]{2,0,1:T(4,128)} %bitcast.12), calls=%async_computation.1 | async-start | bytes 131072 | tf_op jit(solution)/shard_map/all_to_all | solution.py:339

commit v3 on v2

--- a/solution.py
+++ b/solution.py
@@ -131,15 +131,20 @@
     values, slopes = spline(position - lowest)
     cell = lax.broadcasted_iota(jnp.int32, (length, position.shape[1]), 0)
     step = (cell - (lowest.astype(jnp.int32) - 1)) & (length - 1)
-    hits = [step == offset for offset in range(4)]
+    step = step.astype(jnp.int16)
+    hits = [step == jnp.asarray(offset, step.dtype) for offset in range(4)]
 
     def dense(members):
-        out = jnp.zeros(step.shape, jnp.float32)
+        out = jnp.zeros(step.shape, jnp.bfloat16)
         for offset in range(4):
             out = jnp.where(hits[offset], members[offset], out)
         return out
 
-    return (dense(values), dense(slopes)) if with_slope else (dense(values),)
+    def both(members):
+        halves = [split(member) for member in members]
+        return dense([half[0] for half in halves]), dense([half[1] for half in halves])
+
+    return (both(values), both(slopes)) if with_slope else (both(values),)
 
 
 def mesh_kernel(chunks, group, fields, rxh, rxl, ryh, ryl, rzh, rzl, screen, out, total, gh, gl, xs, xd):
@@ -152,7 +157,7 @@
     nt = ((1,), (1,))
 
     def along(high, low, dense):
-        return dot3((high[...], low[...]), split(dense), nn)
+        return dot3((high[...], low[...]), dense, nn)
 
     @pl.when(step == 0)
     def _():
@@ -171,7 +176,7 @@
             total[where, :] += dot3(pair, zs, nt)
             return carry
 
-        lax.fori_loop(0, nx // group, body, 0)
+        lax.fori_loop(0, nx // group, body, 0, unroll=True)
 
     @pl.when(step == chunks - 1)
     def _():
@@ -213,7 +218,7 @@
             return force_x, force_y, force_z
 
         empty = jnp.zeros((1, atoms), jnp.float32)
-        found = lax.fori_loop(0, nx // group, body, (empty, empty, empty))
+        found = lax.fori_loop(0, nx // group, body, (empty, empty, empty), unroll=True)
         for c in range(3):
             out[c : c + 1, :] = -fields[0:1, :] * found[c]
 

time: 131 us -> 118 us (0.901)
  Pallas kernels: 86.2 us -> 73.8 us
    pallas_call x1, Pallas kernels: 77.6 us -> 65.1 us  [mesh_forces(): pl.pallas_call(functools.partial(mesh_kernel, chunks, group), grid=(2 * c...]
where the time goes in v3:
time: 118 us
  Pallas kernels  73.8 us (63%)
  blocking collectives  13.6 us (12%)
  starting transfers between devices  13.4 us (11%)
  waiting for transfers between devices  5.74 us (5%)
  other arithmetic  5.44 us (5%)
  local copies, waits for them, and re-layouts  3.84 us (3%)
    pallas_call x1, Pallas kernels, mesh_forces(): pl.pallas_call(functools.partial(mesh_kernel, chunks, group), grid=(2 * c...  65.1 us
    pallas_call x1, Pallas kernels, kick_short(): pl.pallas_call(pair_kernel, out_shape=jax.ShapeDtypeStruct(momenta.shape,...  8.67 us
    all_gather x1, blocking collectives, per_device(): lax.all_gather(jnp.stack([positions, kicked, noise]), 'bead', axis=2, til...  7.53 us
    all_to_all x1, starting transfers between devices, per_device(): lax.all_to_all(copies, 'grid', split_axis=1, concat_axis=1, tiled=True)  7.44 us
    psum x1, blocking collectives, per_device(): mesh_force = half_step * lax.psum(jnp.sum(shares, axis=1), 'bead')  6.08 us
    all_to_all x1, starting transfers between devices, per_device(): lax.all_to_all(partial.reshape(3, grid_count, charges.shape[0]), 'grid',...  6 us
    all_to_all x1, waiting for transfers between devices, per_device(): lax.all_to_all(partial.reshape(3, grid_count, charges.shape[0]), 'grid',...  5.74 us
    dynamic_slice x6, local copies, waits for them, and re-layouts, rows_of(): return lax.dynamic_slice_in_dim(jnp.asarray(values), first, count, 0)  3.03 us
  transfers between devices with their start and end apart: 2, of which 1 were waited for; matrix products, arithmetic and copies ran while one was open for 6% of the time, Pallas kernels for 7%

profile of v3, /device:TPU:0, one launch (start us, length us, event | category | flops | bytes accessed | tf_op | source)
XLA Modules:
  0.0 117.7 jit_solution(10859071334905215259)
XLA Ops:
  0.6 0.8 fusion.12
  1.5 0.7 pad_maximum_fusion.1
  2.2 0.6 broadcast_in_dim.9
  2.8 0.0 copy-start.2
  2.8 0.0 copy-start.3
  2.8 7.4 %all-to-all-start = ((f32[4,8,512]{2,0,1:T(4,128)}), f32[4,8,512]{2,0,1:T(4,128)S(1)}, u32[]{:S(2)}, u32[]{:S(2)}) async-start(f32[4,8,512]{2,0,1:T(4,128)} %broadcast_in_dim.9), calls=%async_computation | async-start | bytes 131072 | tf_op jit(solution)/shard_map/all_to_all | solution.py:341
  10.2 0.8 dynamic_slice.33
  11.0 0.8 dynamic_slice.32
  11.8 0.8 dynamic_slice.35
  12.5 0.8 dynamic_slice.34
  13.3 0.1 broadcast_add_fusion
  13.3 0.1 add.92
  13.4 0.1 broadcast_multiply_fusion
  13.5 0.1 mul.98
  13.5 0.8 convert_reduce_fusion
  14.3 0.6 broadcast_multiply_fusion.3.counts
  14.9 0.0 copy-start.4
  14.9 0.0 copy-start.5
  14.9 8.7 %shard_map.212 = f32[3,8,512]{2,1,0:T(8,128)} custom-call(f32[4,4]{1,0:T(4,128)} %broadcast_multiply_fusion.3.counts, f32[3,8,512]{2,1,0:T(8,128)} %places.1, f32[3,8,512]{2,1,0:T(8,128)} %momenta.1), custom_call_target="tpu_custom_call" | custom-call | flops 41943040 | bytes 147456 | tf_op jit(solution)/shard_map/pallas_call | solution.py:82
  23.6 0.0 copy-start
  23.6 0.0 copy-start.1
  23.6 0.0 copy-done.2
  23.6 0.0 copy-done.3
  23.6 0.9 pad_maximum_fusion
  24.4 7.5 %all_gather.3 = f32[3,3,32,512]{3,2,1,0:T(8,128)S(1)} all-gather(f32[3,3,8,512]{3,2,1,0:T(8,128)S(1)} %pad_maximum_fusion), channel_id=1, replica_groups=mesh['grid'=8,'bead'=4] {'bead'}, dimensions={2}, use_global_device_ids=true | all-gather | bytes 737280 | tf_op jit(solution)/shard_map/all_gather | solution.py:350
  32.0 0.0 copy-done.4
  32.0 0.0 copy-done.5
  32.0 0.9 fusion.1.screen
  32.9 0.0 copy-done
  32.9 0.0 copy-done.1
  32.9 0.0 all-to-all-done
  33.0 65.1 %shard_map.213 = f32[3,4096]{1,0:T(4,128)} custom-call(f32[4,4096]{1,0:T(4,128)S(1)} %bitcast.32, bf16[32,256]{1,0:T(8,128)(2,1)S(1)} %get-tuple-element.10.rxh, bf16[32,256]{1,0:T(8,128)(2,1)S(1)} %get-tuple-element.9.rxl, bf16[64,256]{1,0:T(8,128)(2,1)S(1)} %get-tuple-element.12.ryh, bf16[64,256]{1,0:T(8,128)(2,1)S(1)} %get-tuple-element.11.ryl, ...), custom_call_target="tpu_custom_call" | custom-call | flops 38654705664 | bytes 4194304 | tf_op jit(solution)/shard_map/pallas_call | solution.py:261
  98.0 6.0 %all-to-all-start.1 = ((f32[3,8,512]{2,0,1:T(4,128)}), f32[3,8,512]{2,0,1:T(4,128)S(1)}, u32[]{:S(2)}, u32[]{:S(2)}) async-start(f32[3,8,512]{2,0,1:T(4,128)} %bitcast.12), calls=%async_computation.1 | async-start | bytes 131072 | tf_op jit(solution)/shard_map/all_to_all | solution.py:344
  104.0 1.2 convolution_bitcast_fusion
  105.2 5.7 %all-to-all-done.1 = f32[3,8,512]{2,0,1:T(4,128)S(1)} async-done(((f32[3,8,512]{2,0,1:T(4,128)}), f32[3,8,512]{2,0,1:T(4,128)S(1)}, u32[]{:S(2)}, u32[]{:S(2)}) %all-to-all-start.1) | async-done | bytes 49184 | tf_op jit(solution)/shard_map/all_to_all | solution.py:344
  111.0 6.1 %psum.7 = f32[3,512]{1,0:T(4,128)S(1)} all-reduce(f32[3,512]{1,0:T(4,128)S(1)} %reduce_sum.19), channel_id=1, replica_groups=mesh['grid'=8,'bead'=4] {'bead'}, use_global_device_ids=true, to_apply=%region_2.3 | all-reduce | flops 1536 | bytes 12288 | tf_op jit(solution)/shard_map/psum | solution.py:347
  117.1 0.6 fusion.7
  (4 shorter events, 0.1 us)
Async XLA Ops:
  2.8 20.8 %copy-start.2 = (f32[3,8,512]{2,1,0:T(8,128)S(1)}, f32[3,8,512]{2,1,0:T(8,128)}, u32[]{:S(2)}) copy-start(f32[3,8,512]{2,1,0:T(8,128)} %param.23) | copy-start | bytes 147460
  2.8 20.8 %copy-start.3 = (f32[3,8,512]{2,1,0:T(8,128)S(1)}, f32[3,8,512]{2,1,0:T(8,128)}, u32[]{:S(2)}) copy-start(f32[3,8,512]{2,1,0:T(8,128)} %places.1) | copy-start | bytes 147460
  2.8 30.1 %all-to-all-start = ((f32[4,8,512]{2,0,1:T(4,128)}), f32[4,8,512]{2,0,1:T(4,128)S(1)}, u32[]{:S(2)}, u32[]{:S(2)}) async-start(f32[4,8,512]{2,0,1:T(4,128)} %broadcast_in_dim.9), calls=%async_computation | async-start | bytes 131072 | tf_op jit(solution)/shard_map/all_to_all | solution.py:341
  14.9 17.1 %copy-start.4 = (f32[256]{0:T(256)S(1)}, f32[256]{0:T(256)}, u32[]{:S(2)}) copy-start(f32[256]{0:T(256)} %constant.51.clone) | copy-start | bytes 3076
  14.9 17.1 %copy-start.5 = (f32[256]{0:T(256)S(1)}, f32[256]{0:T(256)}, u32[]{:S(2)}) copy-start(f32[256]{0:T(256)} %constant.52.clone) | copy-start | bytes 3076
  23.6 9.3 %copy-start = (bf16[256,256]{1,0:T(8,128)(2,1)S(1)}, bf16[256,256]{1,0:T(8,128)(2,1)}, u32[]{:S(2)}) copy-start(bf16[256,256]{1,0:T(8,128)(2,1)} %constant.49.clone.rzh) | copy-start | bytes 393220
  23.6 9.3 %copy-start.1 = (bf16[256,256]{1,0:T(8,128)(2,1)S(1)}, bf16[256,256]{1,0:T(8,128)(2,1)}, u32[]{:S(2)}) copy-start(bf16[256,256]{1,0:T(8,128)(2,1)} %constant.50.clone.rzl) | copy-start | bytes 393220
  98.0 12.9 %all-to-all-start.1 = ((f32[3,8,512]{2,0,1:T(4,128)}), f32[3,8,512]{2,0,1:T(4,128)S(1)}, u32[]{:S(2)}, u32[]{:S(2)}) async-start(f32[3,8,512]{2,0,1:T(4,128)} %bitcast.12), calls=%async_computation.1 | async-start | bytes 131072 | tf_op jit(solution)/shard_map/all_to_all | solution.py:344
